TPU v7x, 32 devices: a whole 2x2x4 slice. The times are simulated.
32 devices in a mesh: grp: 2 (over x), seq: 8 (over z, y), pool: 2 (over core).
Axes of the slice: x: 2, y: 2, z: 4, core: 2. Of those that a mesh axis runs over, the one named last changes fastest.
Arguments:
- factors: bfloat16 [2, 65536, 160], P('grp', 'seq'), parts along dimension 0, may hold values from -6 to 6
- basis: bfloat16 [2, 160, 1024], P('grp', None, 'pool'), parts along dimension 0, may hold values from -1 to 1
- value_pool: bfloat16 [2, 65536, 1024], P('grp', ('seq', 'pool')), parts along dimension 0, may hold values from -6 to 6
- page_summary: bfloat16 [2, 8192, 1024], P('grp', 'seq', 'pool'), parts along dimension 0, may hold values from -6 to 6
- recent_keys: bfloat16 [2, 64, 1024], P('grp', None, 'pool'), parts along dimension 0, may hold values from -20 to 20
- recent_values: bfloat16 [2, 64, 1024], P('grp', None, 'pool'), parts along dimension 0, may hold values from -6 to 6
- query: bfloat16 [2, 8192], P('grp', 'pool'), parts along dimension 0, may hold values from -8192 to 8192
- selected: int32 [2, 8, 1024], P('grp'), parts along dimension 0, may hold values from 0 to 8191, as said below
- owner_map: int32 [2, 8192], P('grp', 'seq'), parts along dimension 0, may hold values from 0 to 1, as said below
- lengths: int32 [2], P('grp'), parts along dimension 0, may hold values from 32768 to 65536, as said below
Outputs:
- attn: bfloat16 [2, 8192], P('grp', 'pool'), parts along dimension 0
There are 2 independent parts, one for each index of `grp`. A program takes and returns all parts, laid end to end along the dimension named above; each array names one. Nothing has to cross between parts.
Inputs may be any that keep to these rules, and one draw needn't show every extreme that they name: `selected`: for every request and key-value head, 1024 distinct page ids in ascending order, each below ceil(lengths / 8); every aligned block of 1024 pages holds at most 256 of them, and for every request and head some block holds exactly 256. `owner_map`: in every aligned block of 1024 pages of a request exactly half of the pages have owner 1. `lengths`: some request has exactly 65536 tokens.
All inputs are finite; a program needn't handle non-finite values.
Results may differ from a plain program's by a relative error of at most 0.0075.
The roundings to bfloat16 on the way count: a program that leaves them out, or rounds other values in their place, can miss the bound.
Values may be sent and summed in bfloat16 or wider, within the bound.
A program may use at most 128 MiB of HBM per device.

v0:
```python
import math

import jax
import jax.numpy as jnp
import numpy as np
from jax import lax
from jax.sharding import PartitionSpec as P

HD = 128
PAGE = 8
SEL = 1024
CAPMIN = 64
WIN = 64


def partner(x, axis, apart):
    return lax.ppermute(x, axis, [(i, i ^ 1 << apart) for i in range(lax.axis_size(axis))])


def llama_rates(head_dim):
    half_dim = head_dim // 2
    base_rates = 500000.0 ** (-(np.arange(half_dim) * 2.0) / head_dim)
    wavelen = 2.0 * math.pi / base_rates
    smooth = (8192.0 / wavelen - 1.0) / 3.0
    blended = (1.0 - smooth) * base_rates / 8.0 + smooth * base_rates
    return np.where(
        wavelen < 2048.0, base_rates, np.where(wavelen > 8192.0, base_rates / 8.0, blended)
    )


def angle_tables(length, head_dim):
    inv_rates = llama_rates(head_dim)
    coarse = (np.arange(length // 256) * 256.0)[:, None] * inv_rates[None, :]
    fine_angles = (np.arange(256) * 1.0)[:, None] * inv_rates[None, :]
    return (np.cos(coarse), np.sin(coarse), np.cos(fine_angles), np.sin(fine_angles))


def combine_angles(coarse_cos, coarse_sin, fine_cos, fine_sin):
    cosine = (
        coarse_cos[:, None, :] * fine_cos[None, :, :]
        - coarse_sin[:, None, :] * fine_sin[None, :, :]
    )
    sine_table = (
        coarse_sin[:, None, :] * fine_cos[None, :, :]
        + coarse_cos[:, None, :] * fine_sin[None, :, :]
    )
    row_count = coarse_cos.shape[0] * 256
    return (cosine.reshape(row_count, -1), sine_table.reshape(row_count, -1))


def rotate(values, cosine, sine_table):
    half_dim = values.shape[-1] // 2
    first_half = values[..., :half_dim]
    second_half = values[..., half_dim:]
    return jnp.concatenate(
        [
            first_half * cosine - second_half * sine_table,
            second_half * cosine + first_half * sine_table,
        ],
        axis=-1,
    )


def slot_pages(chosen_ids, first_page, pages_dev, capacity):
    before = jnp.sum((chosen_ids < first_page).astype(jnp.int32), axis=-1)
    inside = jnp.sum(
        ((chosen_ids >= first_page) & (chosen_ids < first_page + pages_dev)).astype(jnp.int32),
        axis=-1,
    )
    filler = jnp.zeros(chosen_ids.shape[:-1] + (capacity,), jnp.int32) + first_page
    padded = jnp.concatenate([chosen_ids, filler], axis=-1)
    offsets = before[..., None] + jnp.arange(capacity, dtype=jnp.int32)
    picked = jnp.take_along_axis(padded, offsets, axis=-1)
    slot_live = jnp.arange(capacity, dtype=jnp.int32) < inside[..., None]
    return (jnp.where(slot_live, picked - first_page, 0), slot_live)


def merge_parts(earlier, following):
    peak_a, sum_a, out_a = earlier
    peak_b, sum_b, out_b = following
    joint_peak = jnp.maximum(peak_a, peak_b)
    factor_a = jnp.exp(peak_a - joint_peak)
    factor_b = jnp.exp(peak_b - joint_peak)
    return (
        joint_peak,
        sum_a * factor_a + sum_b * factor_b,
        out_a * factor_a[..., None] + out_b * factor_b[..., None],
    )


def local(
    factors,
    basis,
    value_pool,
    page_summary,
    recent_keys,
    recent_values,
    query,
    selected,
    owner_map,
    lengths,
):
    requests, span_rows, rank_dim = factors.shape
    seq_count = lax.axis_size("seq")
    seq_pos = lax.axis_index("seq")
    core_index = lax.axis_index("pool")
    heads_here = basis.shape[2] // HD
    group_size = query.shape[1] // (heads_here * HD)
    pages_dev = span_rows // PAGE
    half_pages = pages_dev // 2
    capacity = max(CAPMIN, 2 * SEL // seq_count)
    score_scale = HD ** (-0.5)
    first_token = seq_pos * span_rows
    first_page = seq_pos * pages_dev
    tables = angle_tables(span_rows * seq_count, HD)
    blocks = span_rows // 256
    coarse_cos = lax.dynamic_slice_in_dim(
        jnp.asarray(tables[0], jnp.float32), seq_pos * blocks, blocks, 0
    )
    coarse_sin = lax.dynamic_slice_in_dim(
        jnp.asarray(tables[1], jnp.float32), seq_pos * blocks, blocks, 0
    )
    cosine, sine_table = combine_angles(
        coarse_cos,
        coarse_sin,
        jnp.asarray(tables[2], jnp.float32),
        jnp.asarray(tables[3], jnp.float32),
    )
    stacked = jnp.einsum("rtk,rkc->rtc", factors, basis, preferred_element_type=jnp.float32)
    stacked = stacked.reshape(requests, span_rows, heads_here, HD)
    keys_bf = rotate(stacked, cosine[None, :, None, :], sine_table[None, :, None, :]).astype(
        jnp.bfloat16
    )
    positions = first_token + jnp.arange(span_rows, dtype=jnp.int32)
    in_range = positions[None, :] < lengths[:, None]
    page_valid = in_range.reshape(requests, pages_dev, PAGE)
    any_valid = jnp.any(page_valid, axis=2)
    paged_keys = keys_bf.reshape(requests, pages_dev, PAGE, heads_here, HD)
    token_mask = page_valid[:, :, :, None, None]
    low_keys = jnp.min(jnp.where(token_mask, paged_keys, jnp.inf), axis=2)
    high_keys = jnp.max(jnp.where(token_mask, paged_keys, -jnp.inf), axis=2)
    center = jnp.where(
        any_valid[:, :, None, None],
        (low_keys.astype(jnp.float32) + high_keys.astype(jnp.float32)) * 0.5,
        0.0,
    ).astype(jnp.bfloat16)
    queries = query.reshape(requests, heads_here, group_size, HD)
    request_idx = jnp.arange(requests, dtype=jnp.int32)[:, None, None]
    local_heads = jnp.arange(heads_here, dtype=jnp.int32)
    my_heads = (core_index * heads_here + local_heads)[None, :, None]
    other_heads = ((1 - core_index) * heads_here + local_heads)[None, :, None]
    ones_count = jnp.cumsum(owner_map, axis=1)
    zeros_count = jnp.cumsum(1 - owner_map, axis=1)
    page_rank = jnp.where(owner_map == 1, ones_count, zeros_count) - 1
    my_ids = lax.dynamic_slice_in_dim(selected, core_index * heads_here, heads_here, 1)
    other_ids = lax.dynamic_slice_in_dim(selected, (1 - core_index) * heads_here, heads_here, 1)
    my_local, my_live = slot_pages(my_ids, first_page, pages_dev, capacity)
    other_local, other_live = slot_pages(other_ids, first_page, pages_dev, capacity)
    my_owner = owner_map[request_idx, my_local]
    my_rank = page_rank[request_idx, my_local]
    other_owner = owner_map[request_idx, other_local]
    other_rank = page_rank[request_idx, other_local]
    held_here = my_owner == core_index
    other_held = (other_owner == core_index) & other_live
    key_rows = paged_keys[request_idx, my_local, :, local_heads[None, :, None], :]
    exact_scores = (
        jnp.einsum("rhgd,rhcpd->rhgcp", queries, key_rows, preferred_element_type=jnp.float32)
        * score_scale
    )
    token_pos = first_token + my_local[..., None] * PAGE + jnp.arange(PAGE, dtype=jnp.int32)
    exact_ok = my_live[..., None] & (token_pos < lengths[:, None, None, None])
    exact_scores = jnp.where(exact_ok[:, :, None], exact_scores, -jnp.inf)
    chosen_mask = jnp.any(
        (my_local[..., None] == jnp.arange(pages_dev, dtype=jnp.int32)) & my_live[..., None], axis=2
    )
    land_scores = (
        jnp.einsum("rhgd,rphd->rhgp", queries, center, preferred_element_type=jnp.float32)
        * score_scale
    )
    land_ok = any_valid[:, None, :] & jnp.logical_not(chosen_mask)
    land_scores = jnp.where(land_ok[:, :, None, :], land_scores, -jnp.inf)
    row_peak = jnp.maximum(
        jnp.maximum(jnp.max(exact_scores, axis=(3, 4)), jnp.max(land_scores, axis=3)), -1e30
    )
    exact_w = jnp.exp(exact_scores - row_peak[..., None, None])
    land_w = jnp.exp(land_scores - row_peak[..., None])
    weight_sum = jnp.sum(exact_w, axis=(3, 4)) + jnp.sum(land_w, axis=3)
    exact_b = exact_w.astype(jnp.bfloat16)
    land_b = land_w.astype(jnp.bfloat16)
    summary = page_summary.reshape(requests, pages_dev, heads_here, HD)
    partial_value = jnp.einsum(
        "rhgp,rphd->rhgd", land_b, summary, preferred_element_type=jnp.float32
    )
    value_store = value_pool.reshape(requests, half_pages, PAGE, value_pool.shape[2] // HD, HD)
    local_rows = value_store[request_idx, my_rank, :, my_heads, :]
    outgoing_rows = value_store[request_idx, other_rank, :, other_heads, :]
    outgoing = jnp.where(other_held[..., None, None], outgoing_rows, jnp.zeros_like(outgoing_rows))
    incoming = partner(outgoing, "pool", 0)
    value_rows = jnp.where(held_here[..., None, None], local_rows, incoming)
    partial_value = partial_value + jnp.einsum(
        "rhgcp,rhcpd->rhgd", exact_b, value_rows, preferred_element_type=jnp.float32
    )
    recent_k = recent_keys.reshape(requests, WIN, heads_here, HD)
    recent_v = recent_values.reshape(requests, WIN, heads_here, HD)
    recent_scores = (
        jnp.einsum("rhgd,rwhd->rhgw", queries, recent_k, preferred_element_type=jnp.float32)
        * score_scale
    )
    recent_peak = jnp.max(recent_scores, axis=3)
    recent_w = jnp.exp(recent_scores - recent_peak[..., None])
    recent_sum = jnp.sum(recent_w, axis=3)
    recent_out = jnp.einsum(
        "rhgw,rwhd->rhgd",
        recent_w.astype(jnp.bfloat16),
        recent_v,
        preferred_element_type=jnp.float32,
    )
    row_total = requests * heads_here * group_size
    row_share = row_total // seq_count
    got_peak, got_sum, got_out = (
        lax.all_to_all(
            row_peak.reshape(1, row_total), "seq", split_axis=1, concat_axis=0, tiled=True
        ),
        lax.all_to_all(
            weight_sum.reshape(1, row_total), "seq", split_axis=1, concat_axis=0, tiled=True
        ),
        lax.all_to_all(
            partial_value.reshape(1, row_total, HD), "seq", split_axis=1, concat_axis=0, tiled=True
        ),
    )
    joint_peak = jnp.max(got_peak, axis=0)
    factor = jnp.exp(got_peak - joint_peak[None, :])
    summed = jnp.sum(got_sum * factor, axis=0)
    gathered_out = jnp.sum(got_out * factor[..., None], axis=0)
    row_start = seq_pos * row_share
    mine_peak = lax.dynamic_slice_in_dim(recent_peak.reshape(row_total), row_start, row_share, 0)
    mine_sum = lax.dynamic_slice_in_dim(recent_sum.reshape(row_total), row_start, row_share, 0)
    mine_out = lax.dynamic_slice_in_dim(recent_out.reshape(row_total, HD), row_start, row_share, 0)
    final_peak, final_sum, final_out = merge_parts(
        (joint_peak, summed, gathered_out), (mine_peak, mine_sum, mine_out)
    )
    rows_out = (final_out / final_sum[:, None]).astype(jnp.bfloat16)
    all_rows = lax.all_gather(rows_out, "seq", axis=0, tiled=True)
    return all_rows.reshape(requests, heads_here * group_size * HD)


def solution(mesh):
    placed = (
        P("grp", "seq", None),
        P("grp", None, "pool"),
        P("grp", ("seq", "pool"), None),
        P("grp", "seq", "pool"),
        P("grp", None, "pool"),
        P("grp", None, "pool"),
        P("grp", "pool"),
        P("grp", None, None),
        P("grp", "seq"),
        P("grp"),
    )
    return jax.shard_map(
        local, mesh=mesh, in_specs=placed, out_specs=P("grp", "pool"), check_vma=False
    )
```

profile of v0, /device:TPU:0, one launch (start us, length us, event | category | flops | bytes accessed | tf_op | source)
XLA Modules:
  0.0 208.9 jit_solution(5469197252403658698)
XLA Ops:
  1.2 9.1 %gather_fusion.7 = s32[1024]{0:T(1024)S(1)} fusion(s32[4,1280]{1,0:T(4,128)S(1)} %get-tuple-element.43, s32[1024]{0:T(1024)S(1)} %bitcast.168), kind=kCustom, calls=%fused_computation.clone | custom fusion | bytes 16384 | tf_op jit(solution)/shard_map/jit(take_along_axis)/gather | solution.py:73
  11.9 9.1 %gather_fusion.8 = s32[1024]{0:T(1024)S(1)} fusion(s32[4,1280]{1,0:T(4,128)S(1)} %get-tuple-element.42, s32[1024]{0:T(1024)S(1)} %bitcast.169), kind=kCustom, calls=%fused_computation.1.clone | custom fusion | bytes 16384 | tf_op jit(solution)/shard_map/jit(take_along_axis)/gather | solution.py:73
  21.1 6.5 %gather_fusion.4 = s32[1024]{0:T(1024)S(1)} fusion(s32[1,1024]{1,0:T(1,128)S(1)} %copy-done.2, s32[1024]{0:T(1024)S(1)} %bitcast.163), kind=kCustom, calls=%fused_computation.6 | custom fusion | bytes 16384 | tf_op jit(solution)/shard_map/gather | solution.py:161
  27.7 6.5 %gather_fusion.5 = s32[1024]{0:T(1024)S(1)} fusion(s32[1,1024]{1,0:T(1,128)S(1)} %fusion.47, s32[1024]{0:T(1024)S(1)} %bitcast.164), kind=kCustom, calls=%fused_computation.7 | custom fusion | bytes 16384 | tf_op jit(solution)/shard_map/gather | solution.py:162
  34.2 6.5 %gather_fusion.2 = s32[1024]{0:T(1024)S(1)} fusion(s32[1,1024]{1,0:T(1,128)S(1)} %fusion.47, s32[1024]{0:T(1024)S(1)} %bitcast.161), kind=kCustom, calls=%fused_computation.4 | custom fusion | bytes 16384 | tf_op jit(solution)/shard_map/gather | solution.py:160
  41.0 12.5 %gather_fusion.6 = bf16[1024,8,128]{2,1,0:T(8,128)(2,1)} fusion(bf16[1,512,8,8,128]{4,2,3,1,0:T(8,128)(2,1)} %bitcast.178, s32[1024]{0:T(1024)S(1)} %bitcast.166), kind=kCustom, calls=%fused_computation.8 | custom fusion | bytes 4206592 | tf_op jit(solution)/shard_map/gather | solution.py:196
  53.5 4.5 %broadcast_select_fusion = bf16[1,4,256,8,128]{4,3,2,1,0:T(8,128)(2,1)} fusion(bf16[1,4,256,8,128]{4,3,2,1,0:T(8,128)(2,1)} %bitcast.174, pred[4,256]{1,0:T(4,128)(4,1)S(1)} %fusion.84), kind=kLoop, calls=%fused_computation.26 | loop fusion | flops 1048576 | bytes 4195328 | tf_op jit(solution)/shard_map/jit(_where)/select_n | solution.py:197
  66.7 5.9 %subtract_convert_fusion = (bf16[1,8192,4,64]{1,3,2,0:T(8,128)(2,1)}, bf16[1,8192,4,64]{1,3,2,0:T(8,128)(2,1)}) fusion(f32[1,8192,4,128]{1,3,2,0:T(8,128)S(1)} %convolution_bitcast_fusion, f32[8192,64]{0,1:T(8,128)} %bitcast.173, f32[8192,64]{0,1:T(8,128)} %bitcast.172), kind=kLoop, calls=%fused_computation.14 | loop fusion | flops 16777216 | bytes 29360128 | tf_op jit(solution)/shard_map/convert.3
  72.6 8.4 %copy.71 = bf16[1,8192,4,64]{3,1,2,0:T(8,128)(2,1)} copy(bf16[1,8192,4,64]{1,3,2,0:T(8,128)(2,1)} %get-tuple-element.22) | data formatting | bytes 8388608 | tf_op jit(solution)/shard_map/convert.2
  81.0 8.5 %copy.70 = bf16[1,8192,4,64]{3,1,2,0:T(8,128)(2,1)} copy(bf16[1,8192,4,64]{1,3,2,0:T(8,128)(2,1)} %get-tuple-element.21) | data formatting | bytes 8388608 | tf_op jit(solution)/shard_map/convert.3
  91.3 22.4 %select_reduce_fusion.1 = (bf16[1024,4,128]{2,1,0:T(4,128)(2,1)S(1)}, bf16[1024,4,128]{2,1,0:T(4,128)(2,1)S(1)}, bf16[1,1024,8,4,128]{4,2,3,1,0:T(8,128)(2,1)}) fusion(pred[1024,8]{1,0:T(8,128)(4,1)S(1)} %copy.68, bf16[1,1024,8,4,64]{4,2,1,3,0:T(8,128)(2,1)} %bitcast.170, bf16[1,1024,8,4,64]{4,2,1,3,0:T(8,128)(2,1)} %bitcast.171), kind=kLoop, calls=%fused_computation.12 | loop fusion | flops 32505856 | bytes 18882560 | tf_op jit(solution)/shard_map/reduce_min | solution.py:140
  113.8 4.5 %select_convert_fusion = bf16[1024,4,128]{2,1,0:T(4,128)(2,1)} fusion(bf16[1024,4,128]{2,1,0:T(4,128)(2,1)S(1)} %get-tuple-element.7, bf16[1024,4,128]{2,1,0:T(4,128)(2,1)S(1)} %get-tuple-element.6, pred[1024]{0:T(1024)(128)(4,1)S(1)} %fusion.29), kind=kLoop, calls=%fused_computation.22 | loop fusion | flops 3145728 | bytes 3146752 | tf_op jit(solution)/shard_map/convert_element_type | solution.py:146
  118.3 7.6 %gather_fusion = bf16[1024,8,128]{2,1,0:T(8,128)(2,1)S(1)} fusion(bf16[1,1024,8,4,128]{4,2,3,1,0:T(8,128)(2,1)} %get-tuple-element.23, s32[1024]{0:T(1024)S(1)} %bitcast.165), kind=kCustom, calls=%fused_computation.2 | custom fusion | bytes 4206592 | tf_op jit(solution)/shard_map/gather | solution.py:165
  126.0 2.6 %fusion.40 = f32[4,256,8,8]{3,2,1,0:T(8,128)} fusion(bf16[4,256,8,128]{3,2,1,0:T(8,128)(2,1)S(1)} %bitcast.177, bf16[4096]{0:T(1024)(128)(2,1)S(1)} %reduce.21), kind=kOutput, calls=%fused_computation.83 | convolution fusion | flops 16777216 | bytes 2367488 | tf_op jit(solution)/shard_map/rhgd,rhcpd->rhgcp/dot_general | solution.py:167
  129.1 2.8 %copy.75 = f32[4,256,8,8]{1,2,3,0:T(8,128)S(1)} copy(f32[4,256,8,8]{3,2,1,0:T(8,128)} %fusion.40) | data formatting | bytes 524288 | tf_op jit(solution)/shard_map/rhgd,rhcpd->rhgcp/dot_general | solution.py:167
  133.2 6.8 %all-to-all-start.2 = ((f32[1,8,4]{2,0,1:T(1,128)}), f32[1,8,4]{2,0,1:T(1,128)S(1)}, u32[]{:S(2)}, u32[]{:S(2)}) async-start(f32[1,8,4]{2,0,1:T(1,128)} %bitcast.44), calls=%async_computation.2 | async-start | bytes 8192 | tf_op jit(solution)/shard_map/all_to_all | solution.py:224
  140.0 6.5 %gather_fusion.1 = s32[1024]{0:T(1024)S(1)} fusion(s32[1,1024]{1,0:T(1,128)S(1)} %copy-done.2, s32[1024]{0:T(1024)S(1)} %bitcast.162), kind=kCustom, calls=%fused_computation.3 | custom fusion | bytes 16384 | tf_op jit(solution)/shard_map/gather | solution.py:159
  150.6 12.5 %gather_fusion.3 = bf16[1024,8,128]{2,1,0:T(8,128)(2,1)} fusion(bf16[1,512,8,8,128]{4,2,3,1,0:T(8,128)(2,1)} %bitcast.179, s32[1024]{0:T(1024)S(1)} %bitcast.167), kind=kCustom, calls=%fused_computation.5 | custom fusion | bytes 4206592 | tf_op jit(solution)/shard_map/gather | solution.py:195
  163.1 6.0 %all-to-all-start.1 = ((f32[1,8,4]{2,0,1:T(1,128)}), f32[1,8,4]{2,0,1:T(1,128)S(1)}, u32[]{:S(2)}, u32[]{:S(2)}) async-start(f32[1,8,4]{2,0,1:T(1,128)} %bitcast.41), calls=%async_computation.1 | async-start | bytes 8192 | tf_op jit(solution)/shard_map/all_to_all | solution.py:221
  169.3 6.3 %all-to-all-done.1 = f32[1,8,4]{2,0,1:T(1,128)S(1)} async-done(((f32[1,8,4]{2,0,1:T(1,128)}), f32[1,8,4]{2,0,1:T(1,128)S(1)}, u32[]{:S(2)}, u32[]{:S(2)}) %all-to-all-start.1) | async-done | bytes 160 | tf_op jit(solution)/shard_map/all_to_all | solution.py:221
  175.9 5.5 %fusion.12 = f32[4,8,128]{2,1,0:T(8,128)} fusion(f32[4,8,128]{2,1,0:T(8,128)S(1)} %fusion.15, bf16[4,8,256,8]{3,1,2,0:T(8,128)(2,1)} %copy.77, bf16[1,4,256,8,128]{4,3,2,1,0:T(8,128)(2,1)} %bitcast.180, bf16[1,4,256,8,128]{4,3,2,1,0:T(8,128)(2,1)} %collective-permute-done, pred[4,256]{1,0:T(4,128)(4,1)S(1)} %reshape.1025), kind=kOutput, calls=%fused_computation.33 | convolution fusion | flops 17829888 | bytes 4359168 | tf_op jit(solution)/shard_map/rhgcp,rhcpd->rhgd/dot_general | solution.py:200
  181.4 3.3 %all-to-all-start = ((f32[1,32,128]{2,0,1:T(1,128)}), f32[1,32,128]{2,0,1:T(1,128)S(1)}, u32[]{:S(2)}, u32[]{:S(2)}) async-start(f32[1,32,128]{2,0,1:T(1,128)} %bitcast.39), calls=%async_computation | async-start | bytes 32768 | tf_op jit(solution)/shard_map/all_to_all | solution.py:227
  184.9 6.3 %all-to-all-done = f32[1,32,128]{2,0,1:T(1,128)S(1)} async-done(((f32[1,32,128]{2,0,1:T(1,128)}), f32[1,32,128]{2,0,1:T(1,128)S(1)}, u32[]{:S(2)}, u32[]{:S(2)}) %all-to-all-start) | async-done | bytes 16416 | tf_op jit(solution)/shard_map/all_to_all | solution.py:227
  191.4 16.9 %all-gather = bf16[8,4,128]{2,1,0:T(4,128)(2,1)S(1)} all-gather(bf16[1,4,128]{2,1,0:T(4,128)(2,1)S(1)} %fusion.88), channel_id=1, replica_groups=mesh['grp'=2,'seq'=8,'pool'=2] {'seq'}, dimensions={0}, use_global_device_ids=true | all-gather | bytes 9216 | tf_op jit(solution)/shard_map/all_gather | solution.py:243
  (118 shorter events, 20.4 us)
Async XLA Ops:
  0.0 64.4 %copy-start = (bf16[1,8192,160]{1,2,0:T(8,128)(2,1)S(1)}, bf16[1,8192,160]{1,2,0:T(8,128)(2,1)}, u32[]{:S(2)}) copy-start(bf16[1,8192,160]{1,2,0:T(8,128)(2,1)} %param.16) | copy-start | bytes 7864324
  1.2 9.3 %copy-start.2 = (s32[1,1024]{1,0:T(1,128)S(1)}, s32[1,1024]{1,0:T(1,128)}, u32[]{:S(2)}) copy-start(s32[1,1024]{1,0:T(1,128)} %param.24) | copy-start | bytes 12292
  53.5 5.1 %copy-start.11 = (f32[256,64]{0,1:T(8,128)S(1)}, f32[256,64]{0,1:T(8,128)}, u32[]{:S(2)}) copy-start(f32[256,64]{0,1:T(8,128)} %constant.31.clone) | copy-start | bytes 196612
  53.5 5.1 %copy-start.12 = (f32[256,64]{0,1:T(8,128)S(1)}, f32[256,64]{0,1:T(8,128)}, u32[]{:S(2)}) copy-start(f32[256,64]{0,1:T(8,128)} %constant.32.clone) | copy-start | bytes 196612
  53.5 5.2 %copy-start.6 = (f32[256,64]{0,1:T(8,128)S(1)}, f32[256,64]{0,1:T(8,128)}, u32[]{:S(2)}) copy-start(f32[256,64]{0,1:T(8,128)} %constant.86.clone) | copy-start | bytes 196612
  53.5 5.2 %copy-start.7 = (f32[256,64]{0,1:T(8,128)S(1)}, f32[256,64]{0,1:T(8,128)}, u32[]{:S(2)}) copy-start(f32[256,64]{0,1:T(8,128)} %constant.87.clone) | copy-start | bytes 196612
  58.0 117.9 %collective-permute-start = (bf16[1,4,256,8,128]{4,3,2,1,0:T(8,128)(2,1)}, bf16[1,4,256,8,128]{4,3,2,1,0:T(8,128)(2,1)}, u32[]{:S(2)}, u32[]{:S(2)}) collective-permute-start(bf16[1,4,256,8,128]{4,3,2,1,0:T(8,128)(2,1)} %broadcast_select_fusion), channel_id=1, source_target_pairs={{0,1},{1,0},{2,3},{3,2},{4,5},{5,4},{6,7},{7,6},{8,9},{9,8},{10,11... | collective-permute-start | bytes 6291464 | tf_op jit(solution)/shard_map/ppermute | solution.py:17
  61.8 2.6 %copy-start.5 = (bf16[1,160,512]{2,1,0:T(8,128)(2,1)S(1)}, bf16[1,160,512]{2,1,0:T(8,128)(2,1)}, u32[]{:S(2)}) copy-start(bf16[1,160,512]{2,1,0:T(8,128)(2,1)} %param.17) | copy-start | bytes 491524
  113.7 4.5 %copy-start.10 = (bf16[1,4096]{1,0:T(2,128)(2,1)S(1)}, bf16[1,4096]{1,0:T(2,128)(2,1)}, u32[]{:S(2)}) copy-start(bf16[1,4096]{1,0:T(2,128)(2,1)} %param.22) | copy-start | bytes 24580
  126.0 2.6 %copy-start.4 = (bf16[1024,4,128]{2,1,0:T(4,128)(2,1)S(1)}, bf16[1024,4,128]{2,1,0:T(4,128)(2,1)}, u32[]{:S(2)}) copy-start(bf16[1024,4,128]{2,1,0:T(4,128)(2,1)} %select_convert_fusion) | copy-start | bytes 3145732
  133.2 29.9 %all-to-all-start.2 = ((f32[1,8,4]{2,0,1:T(1,128)}), f32[1,8,4]{2,0,1:T(1,128)S(1)}, u32[]{:S(2)}, u32[]{:S(2)}) async-start(f32[1,8,4]{2,0,1:T(1,128)} %bitcast.44), calls=%async_computation.2 | async-start | bytes 8192 | tf_op jit(solution)/shard_map/all_to_all | solution.py:224
  140.0 7.2 %copy-start.3 = (bf16[1,1024,512]{2,1,0:T(8,128)(2,1)S(1)}, bf16[1,1024,512]{2,1,0:T(8,128)(2,1)}, u32[]{:S(2)}) copy-start(bf16[1,1024,512]{2,1,0:T(8,128)(2,1)} %param.19) | copy-start | bytes 3145732
  146.4 1.0 copy-start.8
  146.5 1.3 copy-start.9
  163.1 12.5 %all-to-all-start.1 = ((f32[1,8,4]{2,0,1:T(1,128)}), f32[1,8,4]{2,0,1:T(1,128)S(1)}, u32[]{:S(2)}, u32[]{:S(2)}) async-start(f32[1,8,4]{2,0,1:T(1,128)} %bitcast.41), calls=%async_computation.1 | async-start | bytes 8192 | tf_op jit(solution)/shard_map/all_to_all | solution.py:221
  175.9 33.0 %copy-start.1 = (bf16[1,8192,160]{1,2,0:T(8,128)(2,1)S(1)}, bf16[1,8192,160]{1,2,0:T(8,128)(2,1)}, u32[]{:S(2)}) copy-start(bf16[1,8192,160]{1,2,0:T(8,128)(2,1)} %param.16) | copy-start | bytes 7864324
  181.4 9.9 %all-to-all-start = ((f32[1,32,128]{2,0,1:T(1,128)}), f32[1,32,128]{2,0,1:T(1,128)S(1)}, u32[]{:S(2)}, u32[]{:S(2)}) async-start(f32[1,32,128]{2,0,1:T(1,128)} %bitcast.39), calls=%async_computation | async-start | bytes 32768 | tf_op jit(solution)/shard_map/all_to_all | solution.py:227
where the time goes:
time: 210 us; the launch traced here: 209 us
  local copies, waits for them, and re-layouts  107 us (51%)
  other arithmetic  42.6 us (20%)
  blocking collectives  16.9 us (8%)
  starting transfers between devices  16.7 us (8%)
  waiting for transfers between devices  12.7 us (6%)
  matrix products  11.7 us (6%)
    reduce_min x1, other arithmetic, local(): low_keys = jnp.min(jnp.where(token_mask, paged_keys, jnp.inf), axis=2)  22.4 us
    gather x4, local copies, waits for them, and re-layouts, slot_pages(): picked = jnp.take_along_axis(padded, offsets, axis=-1)  18.3 us
    another operation x11, local copies, waits for them, and re-layouts  17.5 us
    all_gather x1, blocking collectives, local(): all_rows = lax.all_gather(rows_out, 'seq', axis=0, tiled=True)  16.9 us
    gather x1, local copies, waits for them, and re-layouts, local(): local_rows = value_store[request_idx, my_rank, :, my_heads, :]  12.5 us
    gather x1, local copies, waits for them, and re-layouts, local(): outgoing_rows = value_store[request_idx, other_rank, :, other_heads, :]  12.5 us
    gather x1, local copies, waits for them, and re-layouts, local(): paged_keys[request_idx, my_local, :, local_heads[None, :, None], :]  7.64 us
    all_to_all x1, starting transfers between devices, local(): lax.all_to_all(weight_sum.reshape(1, row_total), 'seq', split_axis=1, con...  6.82 us
  transfers between devices with their start and end apart: 4, of which 2 were waited for; matrix products, arithmetic and copies ran while one was open for 47% of the time, Pallas kernels for 0%

commit v1 on v0

v1 whole, which is shorter than its diff:
```python
import functools
import math

import jax
import jax.numpy as jnp
import numpy as np
from jax import lax
from jax.experimental import pallas as pl
from jax.experimental.pallas import tpu as pltpu
from jax.sharding import PartitionSpec as P

HD = 128
PAGE = 8
WIN = 64
LANES = 128
FINE = 256
GROUP = FINE // PAGE
MESH = pl.DeviceIdType.MESH
BF = jnp.bfloat16
F32 = jnp.float32


def llama_rates(head_dim):
    half_dim = head_dim // 2
    base_rates = 500000.0 ** (-(np.arange(half_dim) * 2.0) / head_dim)
    wavelen = 2.0 * math.pi / base_rates
    smooth = (8192.0 / wavelen - 1.0) / 3.0
    blended = (1.0 - smooth) * base_rates / 8.0 + smooth * base_rates
    return np.where(
        wavelen < 2048.0, base_rates, np.where(wavelen > 8192.0, base_rates / 8.0, blended)
    )


def angle_tables(length, head_dim):
    inv_rates = llama_rates(head_dim)
    coarse = (np.arange(length // FINE) * float(FINE))[:, None] * inv_rates[None, :]
    fine = (np.arange(FINE) * 1.0)[:, None] * inv_rates[None, :]
    order = (np.arange(GROUP)[None, :] * PAGE + np.arange(PAGE)[:, None]).reshape(-1)
    fine = fine[order]
    tables = (np.cos(coarse), np.sin(coarse), np.cos(fine), np.sin(fine))
    return [np.concatenate([t, t], axis=1).astype(np.float32) for t in tables]


def nt(a, b):
    return lax.dot_general(a, b, (((1,), (1,)), ((), ())), preferred_element_type=F32)


def nn(a, b):
    return jnp.dot(a, b, preferred_element_type=F32)


def ones_where(mask):
    return jnp.where(mask, 1.0, 0.0).astype(BF)


def iota(shape, dim):
    return lax.broadcasted_iota(jnp.int32, shape, dim)


def diagonal(wide, heads, gqa):
    return jnp.concatenate(
        [wide[h * gqa : (h + 1) * gqa, h * HD : (h + 1) * HD] for h in range(heads)], axis=0
    )


def local_kernel(
    heads,
    len_ref,
    fac_ref,
    basis_ref,
    sum_ref,
    rk_ref,
    rv_ref,
    q_ref,
    sel_ref,
    own_ref,
    cj_ref,
    sj_ref,
    cm_ref,
    sm_ref,
    w_out,
    acc_out,
    stat_out,
    keys,
    centers,
    scores,
    wbuf,
    onehot,
    grouped,
    perm,
):
    seq_pos = lax.axis_index("seq")
    core = lax.axis_index("pool")
    rows = q_ref.shape[0]
    gqa = rows // heads
    width = heads * HD
    tokens = fac_ref.shape[0]
    pages = tokens // PAGE
    blocks = tokens // FINE
    chunks = pages // LANES
    limit = len_ref[0] - seq_pos * tokens
    scale = HD ** (-0.5)

    new = iota((width, width), 1)
    old = (
        (new // 256 * 2 + new // 64 % 2) * HD + new // 128 % 2 * 64 + new % 64
    )
    col_perm = ones_where(iota((width, width), 0) == old)
    basis = nn(basis_ref[...], col_perm).astype(BF)
    q_wide = jnp.concatenate([q_ref[...].astype(F32)] * heads, axis=1)
    on_diag = iota((rows, width), 0) // gqa == iota((rows, width), 1) // HD
    q_plain = jnp.where(on_diag, q_wide, 0.0).astype(BF)
    q_perm = nn(q_plain, col_perm).astype(BF)
    dst = iota((FINE, FINE), 0)
    tok_perm = ones_where(iota((FINE, FINE), 1) == dst % GROUP * PAGE + dst // GROUP)
    page_row = iota((GROUP, LANES), 0) * PAGE

    def block(j):
        fac = fac_ref[pl.ds(pl.multiple_of(j * FINE, FINE), FINE), :]
        ordered = nn(tok_perm, fac).astype(BF)
        u = nn(ordered, basis)
        cj = cj_ref[pl.ds(seq_pos * blocks + j, 1), :]
        sj = sj_ref[pl.ds(seq_pos * blocks + j, 1), :]
        at = pl.ds(pl.multiple_of(j * GROUP, GROUP), GROUP)
        low = [None] * heads
        high = [None] * heads
        left = limit - j * FINE
        for i in range(PAGE):
            part = slice(i * GROUP, (i + 1) * GROUP)
            cm, sm = cm_ref[part, :], sm_ref[part, :]
            cosine = cj * cm - sj * sm
            sine = sj * cm + cj * sm
            live = page_row + i < left
            for pair in range(heads // 2):
                x = u[part, pair * 256 : pair * 256 + 128]
                y = u[part, pair * 256 + 128 : pair * 256 + 256]
                for k, val in ((0, x * cosine - y * sine), (1, y * cosine + x * sine)):
                    n = pair * 2 + k
                    keys[i, at, n * LANES : (n + 1) * LANES] = val.astype(BF)
                    if i == 0:
                        low[n], high[n] = val, val
                    else:
                        kept = jnp.where(live, val, low[n])
                        low[n] = jnp.minimum(low[n], kept)
                        high[n] = jnp.maximum(high[n], kept)
        any_live = page_row < left
        for n in range(heads):
            mid = (low[n].astype(BF).astype(F32) + high[n].astype(BF).astype(F32)) * 0.5
            centers[at, n * LANES : (n + 1) * LANES] = jnp.where(any_live, mid, 0.0).astype(BF)

    def step(t, carry):
        block(t * 2)
        block(t * 2 + 1)
        return carry

    lax.fori_loop(0, blocks // 2, step, 0)

    sel = jnp.where(core == 0, sel_ref[:heads, :], sel_ref[heads:, :]) - seq_pos * pages
    count = sel.shape[1]
    masks = []
    for h in range(heads):
        ids = sel[h : h + 1, :]
        hi = jnp.floor_divide(ids, LANES)
        lo = ids - hi * LANES
        hit = nt(
            ones_where(iota((8, count), 0) == hi), ones_where(iota((LANES, count), 0) == lo)
        )
        row = jnp.concatenate([hit[c : c + 1, :] for c in range(chunks)], axis=1)
        masks.append(jnp.broadcast_to(row, (gqa, pages)))
    chosen = jnp.concatenate(masks, axis=0) > 0.5
    page_tok = iota((rows, pages), 1) * PAGE
    land = nt(q_perm, centers[...]) * scale
    land = jnp.where((page_tok < limit) & jnp.logical_not(chosen), land, -jnp.inf)
    recent = nt(q_plain, rk_ref[...]) * scale
    first = jnp.zeros(recent.shape, jnp.int32) + seq_pos
    recent = jnp.where(first == 0, recent, -jnp.inf)
    peak = jnp.maximum(jnp.max(land, axis=1, keepdims=True), jnp.max(recent, axis=1, keepdims=True))
    top = jnp.full((rows, pages), -1e30, F32)
    for i in range(PAGE):
        s = nt(q_perm, keys[i]) * scale
        s = jnp.where((page_tok + i < limit) & chosen, s, -jnp.inf)
        scores[i] = s
        top = jnp.maximum(top, s)
    peak = jnp.maximum(peak, jnp.max(top, axis=1, keepdims=True))
    total = jnp.zeros((rows, pages), F32)
    for i in range(PAGE):
        w = jnp.exp(scores[i] - peak)
        total = total + w
        wbuf[i * rows : (i + 1) * rows, :] = w.astype(BF)
    land_w = jnp.exp(land - peak)
    recent_w = jnp.exp(recent - peak)
    row_sum = jnp.sum(total + land_w, axis=1, keepdims=True) + jnp.sum(
        recent_w, axis=1, keepdims=True
    )
    acc_out[...] = diagonal(
        nn(land_w.astype(BF), sum_ref[...]) + nn(recent_w.astype(BF), rv_ref[...]), heads, gqa
    )
    at_lane = iota((rows, LANES), 0) == iota((rows, LANES), 1)
    stat_out[0:1, :] = jnp.sum(jnp.where(at_lane, peak, 0.0), axis=0, keepdims=True)
    stat_out[1:2, :] = jnp.sum(jnp.where(at_lane, row_sum, 0.0), axis=0, keepdims=True)
    stat_out[2:8, :] = jnp.zeros((6, LANES), F32)

    owners = own_ref[...]
    before = nn(
        ones_where(owners == 1), ones_where(iota((LANES, LANES), 0) < iota((LANES, LANES), 1))
    )
    chunk_total = jnp.sum(owners.astype(F32), axis=1, keepdims=True)
    running = jnp.zeros((1, 1), F32)
    slots = []
    for c in range(chunks):
        ones = before[c : c + 1, :] + running
        running = running + chunk_total[c : c + 1, :]
        page = (iota((1, LANES), 1) + c * LANES).astype(F32)
        slots.append(jnp.where(owners[c : c + 1, :] == 1, ones + pages // 2, page - ones))
    slot = jnp.concatenate(slots, axis=1).astype(jnp.int32)
    onehot[...] = ones_where(iota((pages, pages), 0) == slot)
    moved = nt(wbuf[...], onehot[...]).astype(BF)
    for c in range(chunks):
        for i in range(PAGE):
            grouped[c * rows : (c + 1) * rows, i * LANES : (i + 1) * LANES] = moved[
                i * rows : (i + 1) * rows, c * LANES : (c + 1) * LANES
            ]
    span = LANES * PAGE
    col = iota((1, span), 1)
    perm[...] = ones_where(iota((span, span), 0) == col % PAGE * LANES + col // PAGE)
    w_out[...] = nn(grouped[...], perm[...]).astype(BF)


def merge_kernel(
    heads,
    seq_count,
    w_ref,
    acc_ref,
    stat_ref,
    pool_ref,
    out_ref,
    values,
    theirs,
    back_out,
    back_in,
    message,
    gathered,
    v_sem,
    pair_send,
    pair_recv,
    send_sem,
    recv_sem,
):
    seq_pos = lax.axis_index("seq")
    core = lax.axis_index("pool")
    rows = acc_ref.shape[0]
    gqa = rows // heads
    width = heads * HD
    span = LANES * PAGE
    parts = pool_ref.shape[0] // span
    partner = {"pool": 1 - core}

    loads = []
    for g in range(parts):
        load = pltpu.make_async_copy(
            pool_ref.at[pl.ds(g * span, span), :], values.at[pl.ds(g * span, span), :], v_sem.at[g]
        )
        load.start()
        loads.append(load)

    barrier = pltpu.get_barrier_semaphore()
    pl.semaphore_signal(barrier, inc=1, device_id=partner, device_id_type=MESH)
    for k in range(1, seq_count):
        pl.semaphore_signal(
            barrier,
            inc=1,
            device_id={"seq": lax.rem(seq_pos + k, seq_count)},
            device_id_type=MESH,
        )
    pl.semaphore_wait(barrier, seq_count)

    def pair_copy(src, dst, n):
        return pltpu.make_async_remote_copy(
            src_ref=src,
            dst_ref=dst,
            send_sem=pair_send.at[n],
            recv_sem=pair_recv.at[n],
            device_id=partner,
            device_id_type=MESH,
        )

    half = parts * rows
    swap = pair_copy(w_ref.at[pl.ds(pl.multiple_of((1 - core) * half, 32), half), :], theirs, 0)
    swap.start()

    def weighted(weights, columns, g):
        return nn(weights, values[g * span : (g + 1) * span, columns])

    mine = jnp.zeros((rows, width), F32)
    my_cols = pl.ds(pl.multiple_of(core * width, width), width)
    for g in range(parts):
        loads[g].wait()
        w = w_ref[pl.ds(pl.multiple_of(core * half + g * rows, 32), rows), :]
        mine = mine + weighted(w, my_cols, g)
    swap.wait()
    other = jnp.zeros((rows, width), F32)
    other_cols = pl.ds(pl.multiple_of((1 - core) * width, width), width)
    for g in range(parts):
        other = other + weighted(theirs[g * rows : (g + 1) * rows, :], other_cols, g)
    back_out[...] = diagonal(other, heads, gqa)
    back = pair_copy(back_out, back_in, 1)
    back.start()
    part = acc_ref[...] + diagonal(mine, heads, gqa)
    message[rows : rows + 8, :] = stat_ref[...]
    back.wait()
    message[0:rows, :] = part + back_in[...]

    sends = []
    for k in range(1, seq_count):
        send = pltpu.make_async_remote_copy(
            src_ref=message,
            dst_ref=gathered.at[k - 1],
            send_sem=send_sem.at[k - 1],
            recv_sem=recv_sem.at[k - 1],
            device_id={"seq": lax.rem(seq_pos + k, seq_count)},
            device_id_type=MESH,
        )
        send.start()
        sends.append(send)
    for send in sends:
        send.wait()

    peaks = [message[rows : rows + 1, :]]
    sums = [message[rows + 1 : rows + 2, :]]
    for k in range(seq_count - 1):
        peaks.append(gathered[k, rows : rows + 1, :])
        sums.append(gathered[k, rows + 1 : rows + 2, :])
    joint = functools.reduce(jnp.maximum, peaks)
    at_lane = iota((rows, LANES), 0) == iota((rows, LANES), 1)

    def column(row):
        return jnp.sum(jnp.where(at_lane, row, 0.0), axis=1, keepdims=True)

    weight_sum = jnp.zeros((1, LANES), F32)
    mixed = jnp.zeros((rows, LANES), F32)
    for k in range(seq_count):
        factor = jnp.exp(peaks[k] - joint)
        weight_sum = weight_sum + sums[k] * factor
        body = message[0:rows, :] if k == 0 else gathered[k - 1, 0:rows, :]
        mixed = mixed + body * column(factor)
    out_ref[...] = (mixed / column(weight_sum)).astype(BF)


def local(
    seq_count,
    factors,
    basis,
    value_pool,
    page_summary,
    recent_keys,
    recent_values,
    query,
    selected,
    owner_map,
    lengths,
):
    tokens, rank_dim = factors.shape[1:]
    width = basis.shape[2]
    heads = width // HD
    rows = query.shape[1] // HD
    pages = tokens // PAGE
    chunks = pages // LANES
    span = LANES * PAGE
    tables = [jnp.asarray(t) for t in angle_tables(tokens * seq_count, HD)]
    vmem = pl.BlockSpec(memory_space=pltpu.VMEM)
    weights, acc, stats = pl.pallas_call(
        functools.partial(local_kernel, heads),
        out_shape=(
            jax.ShapeDtypeStruct((chunks * rows, span), BF),
            jax.ShapeDtypeStruct((rows, LANES), F32),
            jax.ShapeDtypeStruct((8, LANES), F32),
        ),
        in_specs=[pl.BlockSpec(memory_space=pltpu.SMEM)] + [vmem] * 12,
        out_specs=(vmem, vmem, vmem),
        scratch_shapes=[
            pltpu.VMEM((PAGE, pages, width), BF),
            pltpu.VMEM((pages, width), BF),
            pltpu.VMEM((PAGE, rows, pages), F32),
            pltpu.VMEM((PAGE * rows, pages), BF),
            pltpu.VMEM((pages, pages), BF),
            pltpu.VMEM((chunks * rows, span), BF),
            pltpu.VMEM((span, span), BF),
        ],
        compiler_params=pltpu.CompilerParams(vmem_limit_bytes=60 * 1024 * 1024),
    )(
        lengths,
        factors[0],
        basis[0],
        page_summary[0],
        recent_keys[0],
        recent_values[0],
        query.reshape(rows, HD),
        selected[0],
        owner_map.reshape(chunks, LANES),
        *tables,
    )
    parts = value_pool.shape[1] // span
    out = pl.pallas_call(
        functools.partial(merge_kernel, heads, seq_count),
        out_shape=jax.ShapeDtypeStruct((rows, HD), BF),
        in_specs=[vmem, vmem, vmem, pl.BlockSpec(memory_space=pl.ANY)],
        out_specs=vmem,
        scratch_shapes=[
            pltpu.VMEM(value_pool.shape[1:], BF),
            pltpu.VMEM((parts * rows, span), BF),
            pltpu.VMEM((rows, LANES), F32),
            pltpu.VMEM((rows, LANES), F32),
            pltpu.VMEM((rows + 8, LANES), F32),
            pltpu.VMEM((seq_count - 1, rows + 8, LANES), F32),
            pltpu.SemaphoreType.DMA((parts,)),
            pltpu.SemaphoreType.DMA((2,)),
            pltpu.SemaphoreType.DMA((2,)),
            pltpu.SemaphoreType.DMA((seq_count - 1,)),
            pltpu.SemaphoreType.DMA((seq_count - 1,)),
        ],
        compiler_params=pltpu.CompilerParams(
            collective_id=0, has_side_effects=True, vmem_limit_bytes=40 * 1024 * 1024
        ),
    )(weights, acc, stats, value_pool[0])
    return out.reshape(1, rows * HD)


def solution(mesh):
    placed = (
        P("grp", "seq", None),
        P("grp", None, "pool"),
        P("grp", ("seq", "pool"), None),
        P("grp", "seq", "pool"),
        P("grp", None, "pool"),
        P("grp", None, "pool"),
        P("grp", "pool"),
        P("grp", None, None),
        P("grp", "seq"),
        P("grp"),
    )
    return jax.shard_map(
        functools.partial(local, mesh.shape["seq"]),
        mesh=mesh,
        in_specs=placed,
        out_specs=P("grp", "pool"),
        check_vma=False,
    )
```

time: 210 us -> 47.3 us (0.23)
  local copies, waits for them, and re-layouts: 107 us -> 12.1 us
  other arithmetic: 42.6 us -> 1.36 us
  Pallas kernels: 0 us -> 32.7 us
  blocking collectives: 16.9 us -> 0 us
  starting transfers between devices: 16.7 us -> 0 us
  waiting for transfers between devices: 12.7 us -> 0 us
  matrix products: 11.7 us -> 0 us
    gather x13 -> x0, local copies, waits for them, and re-layouts: 76.7 us -> none  [the longest x4 18.3 us: slot_pages(): picked = jnp.take_along_axis(padded, offsets, axis=-1)]
    pallas_call x0 -> x2, Pallas kernels: none -> 32.7 us  [the longest x1 18.8 us: local(): pl.pallas_call(functools.partial(local_kernel, heads), out_shape=(jax.Sha...]
    reduce_min x1 -> x0, other arithmetic: 22.4 us -> none  [local(): low_keys = jnp.min(jnp.where(token_mask, paged_keys, jnp.inf), axis=2)]
    another operation x12 -> x0, local copies, waits for them, and re-layouts: 17.5 us -> none
    all_gather x1 -> x0, blocking collectives: 16.9 us -> none  [local(): all_rows = lax.all_gather(rows_out, 'seq', axis=0, tiled=True)]
    all_to_all x3 -> x0, starting transfers between devices: 16.1 us -> none  [the longest x1 6.82 us: local(): lax.all_to_all(weight_sum.reshape(1, row_total), 'seq', split_axis=1, con...]
    all_to_all x3 -> x0, waiting for transfers between devices: 12.7 us -> none  [the longest x1 6.34 us: local(): lax.all_to_all(partial_value.reshape(1, row_total, HD), 'seq', split_axis...]
    dot_general x7 -> x0, matrix products: 11.7 us -> none  [the longest x1 5.48 us: local(): jnp.einsum('rhgcp,rhcpd->rhgd', exact_b, value_rows, preferred_element_ty...]
  transfers between devices with their start and end apart: 4 -> 0, of which waited for: 2 -> 0; matrix products, arithmetic and copies ran while one was open for 47% -> 0% of each run, Pallas kernels for 0% -> 0%
where the time goes in v1:
time: 47.3 us; the launch traced here: 46.9 us
  Pallas kernels  32.7 us (69%)
  local copies, waits for them, and re-layouts  12.1 us (26%)
  other arithmetic  1.36 us (3%)
  between operations  0.67 us (1%)
    pallas_call x1, Pallas kernels, local(): pl.pallas_call(functools.partial(local_kernel, heads), out_shape=(jax.Sha...  18.8 us
    pallas_call x1, Pallas kernels, local(): pl.pallas_call(functools.partial(merge_kernel, heads, seq_count), out_sha...  13.9 us
    unnamed x10, local copies, waits for them, and re-layouts  12.1 us
    unnamed x1, other arithmetic  1.36 us

profile of v1, /device:TPU:0, one launch (start us, length us, event | category | flops | bytes accessed | tf_op | source)
XLA Modules:
  0.0 46.9 jit_solution(15165846310949846689)
XLA Ops:
  0.7 1.4 %reduce = bf16[4096]{0:T(1024)(128)(2,1)} reduce(bf16[1,4096]{1,0:T(2,128)(2,1)} %param.20, bf16[]{:T(256)} %constant.22), dimensions={0}, to_apply=%param.20.reduce_sub_computation | reduce | bytes 16386 | tf_op args[6]
  2.0 5.7 %copy.15 = bf16[1,8192,160]{2,1,0:T(8,128)(2,1)} copy(bf16[1,8192,160]{1,2,0:T(8,128)(2,1)} %param.14) | data formatting | bytes 5242880 | tf_op args[0]
  7.7 18.8 %shard_map.136 = (bf16[256,1024]{1,0:T(8,128)(2,1)}, f32[32,128]{1,0:T(8,128)}, f32[8,128]{1,0:T(8,128)}) custom-call(s32[1]{0:T(128)S(6)} %copy.19.len_ref, bf16[8192,160]{1,0:T(8,128)(2,1)} %bitcast.16, bf16[160,512]{1,0:T(8,128)(2,1)} %bitcast.18, bf16[1024,512]{1,0:T(8,128)(2,1)} %bitcast.17, bf16[64,512]{1,0:T(8,128)(2,1)} %bitcast.19, ...), custom_call_target="tpu_custom_call" | custom-call | tf_op jit(solution)/shard_map/pallas_call | solution.py:371
  26.5 0.0 copy-start
  26.5 3.4 %copy-done = bf16[1,4096,1024]{2,1,0:T(8,128)(2,1)S(1)} copy-done((bf16[1,4096,1024]{2,1,0:T(8,128)(2,1)S(1)}, bf16[1,4096,1024]{2,1,0:T(8,128)(2,1)}, u32[]{:S(2)}) %copy-start) | copy-done | bytes 8388632
  29.9 0.0 copy-start.1
  29.9 1.0 %copy-done.1 = bf16[256,1024]{1,0:T(8,128)(2,1)S(1)} copy-done((bf16[256,1024]{1,0:T(8,128)(2,1)S(1)}, bf16[256,1024]{1,0:T(8,128)(2,1)}, u32[]{:S(2)}) %copy-start.1) | copy-done | bytes 524312
  30.9 0.0 copy-start.2
  30.9 0.7 %copy-done.2 = f32[32,128]{1,0:T(8,128)S(1)} copy-done((f32[32,128]{1,0:T(8,128)S(1)}, f32[32,128]{1,0:T(8,128)}, u32[]{:S(2)}) %copy-start.2) | copy-done | bytes 16408
  31.6 0.0 copy-start.3
  31.6 0.7 %copy-done.3 = f32[8,128]{1,0:T(8,128)S(1)} copy-done((f32[8,128]{1,0:T(8,128)S(1)}, f32[8,128]{1,0:T(8,128)}, u32[]{:S(2)}) %copy-start.3) | copy-done | bytes 4120
  32.3 13.9 %shard_map.137 = bf16[32,128]{1,0:T(8,128)(2,1)S(1)} custom-call(bf16[256,1024]{1,0:T(8,128)(2,1)S(1)} %copy-done.1, f32[32,128]{1,0:T(8,128)S(1)} %copy-done.2, f32[8,128]{1,0:T(8,128)S(1)} %copy-done.3, bf16[4096,1024]{1,0:T(8,128)(2,1)S(1)} %bitcast.14), custom_call_target="tpu_custom_call" | custom-call | tf_op jit(solution)/shard_map/pallas_call | solution.py:403
  46.3 0.6 %copy.18 = bf16[1,1,32,128]{3,1,2,0:T(2,128)(2,1)} copy(bf16[1,1,32,128]{3,2,1,0:T(8,128)(2,1)S(1)} %bitcast.15) | data formatting | bytes 16384
Async XLA Ops:
  26.5 3.4 %copy-start = (bf16[1,4096,1024]{2,1,0:T(8,128)(2,1)S(1)}, bf16[1,4096,1024]{2,1,0:T(8,128)(2,1)}, u32[]{:S(2)}) copy-start(bf16[1,4096,1024]{2,1,0:T(8,128)(2,1)} %param.16) | copy-start | bytes 25165828
  29.9 1.0 %copy-start.1 = (bf16[256,1024]{1,0:T(8,128)(2,1)S(1)}, bf16[256,1024]{1,0:T(8,128)(2,1)}, u32[]{:S(2)}) copy-start(bf16[256,1024]{1,0:T(8,128)(2,1)} %get-tuple-element.8.w_ref) | copy-start | bytes 1572868
  30.9 0.7 %copy-start.2 = (f32[32,128]{1,0:T(8,128)S(1)}, f32[32,128]{1,0:T(8,128)}, u32[]{:S(2)}) copy-start(f32[32,128]{1,0:T(8,128)} %get-tuple-element.9.acc_ref) | copy-start | bytes 49156
  31.6 0.7 %copy-start.3 = (f32[8,128]{1,0:T(8,128)S(1)}, f32[8,128]{1,0:T(8,128)}, u32[]{:S(2)}) copy-start(f32[8,128]{1,0:T(8,128)} %get-tuple-element.10.stat_ref) | copy-start | bytes 12292

commit v2 on v1

--- a/solution.py
+++ b/solution.py
@@ -63,12 +63,11 @@
     )
 
 
-def local_kernel(
+def attention_kernel(
     heads,
+    seq_count,
     len_ref,
-    fac_ref,
     basis_ref,
-    sum_ref,
     rk_ref,
     rv_ref,
     q_ref,
@@ -78,9 +77,13 @@
     sj_ref,
     cm_ref,
     sm_ref,
-    w_out,
-    acc_out,
-    stat_out,
+    fac_hbm,
+    sum_hbm,
+    pool_hbm,
+    out_ref,
+    fac,
+    summary,
+    values,
     keys,
     centers,
     scores,
@@ -88,18 +91,59 @@
     onehot,
     grouped,
     perm,
+    outgoing,
+    theirs,
+    back_out,
+    back_in,
+    message,
+    gathered,
+    f_sem,
+    s_sem,
+    v_sem,
+    pair_send,
+    pair_recv,
+    send_sem,
+    recv_sem,
 ):
     seq_pos = lax.axis_index("seq")
     core = lax.axis_index("pool")
-    rows = q_ref.shape[0]
+    rows = q_ref.shape[1] // HD
     gqa = rows // heads
     width = heads * HD
-    tokens = fac_ref.shape[0]
+    tokens = fac.shape[1]
     pages = tokens // PAGE
     blocks = tokens // FINE
     chunks = pages // LANES
+    span = LANES * PAGE
+    parts = values.shape[0] // span
     limit = len_ref[0] - seq_pos * tokens
     scale = HD ** (-0.5)
+    partner = {"pool": 1 - core}
+
+    def fac_load(n):
+        at = pl.ds(pl.multiple_of(n * span, span), span)
+        return pltpu.make_async_copy(fac_hbm.at[:, at], fac.at[:, at], f_sem.at[n])
+
+    for n in range(chunks):
+        fac_load(n).start()
+    sum_load = pltpu.make_async_copy(sum_hbm, summary, s_sem)
+    sum_load.start()
+    loads = []
+    for g in range(parts):
+        at = pl.ds(g * span, span)
+        load = pltpu.make_async_copy(pool_hbm.at[at, :], values.at[at, :], v_sem.at[g])
+        load.start()
+        loads.append(load)
+
+    barrier = pltpu.get_barrier_semaphore()
+    pl.semaphore_signal(barrier, inc=1, device_id=partner, device_id_type=MESH)
+    for k in range(1, seq_count):
+        pl.semaphore_signal(
+            barrier,
+            inc=1,
+            device_id={"seq": lax.rem(seq_pos + k, seq_count)},
+            device_id_type=MESH,
+        )
 
     new = iota((width, width), 1)
     old = (
@@ -107,7 +151,9 @@
     )
     col_perm = ones_where(iota((width, width), 0) == old)
     basis = nn(basis_ref[...], col_perm).astype(BF)
-    q_wide = jnp.concatenate([q_ref[...].astype(F32)] * heads, axis=1)
+    q_flat = q_ref[...].astype(F32)
+    q_rows = jnp.concatenate([q_flat[:, r * HD : (r + 1) * HD] for r in range(rows)], axis=0)
+    q_wide = jnp.concatenate([q_rows] * heads, axis=1)
     on_diag = iota((rows, width), 0) // gqa == iota((rows, width), 1) // HD
     q_plain = jnp.where(on_diag, q_wide, 0.0).astype(BF)
     q_perm = nn(q_plain, col_perm).astype(BF)
@@ -116,8 +162,7 @@
     page_row = iota((GROUP, LANES), 0) * PAGE
 
     def block(j):
-        fac = fac_ref[pl.ds(pl.multiple_of(j * FINE, FINE), FINE), :]
-        ordered = nn(tok_perm, fac).astype(BF)
+        ordered = nt(tok_perm, fac[:, pl.ds(pl.multiple_of(j * FINE, FINE), FINE)]).astype(BF)
         u = nn(ordered, basis)
         cj = cj_ref[pl.ds(seq_pos * blocks + j, 1), :]
         sj = sj_ref[pl.ds(seq_pos * blocks + j, 1), :]
@@ -148,12 +193,15 @@
             mid = (low[n].astype(BF).astype(F32) + high[n].astype(BF).astype(F32)) * 0.5
             centers[at, n * LANES : (n + 1) * LANES] = jnp.where(any_live, mid, 0.0).astype(BF)
 
+    per_chunk = span // FINE
+
     def step(t, carry):
-        block(t * 2)
-        block(t * 2 + 1)
+        fac_load(t).wait()
+        for k in range(per_chunk):
+            block(t * per_chunk + k)
         return carry
 
-    lax.fori_loop(0, blocks // 2, step, 0)
+    lax.fori_loop(0, chunks, step, 0)
 
     sel = jnp.where(core == 0, sel_ref[:heads, :], sel_ref[heads:, :]) - seq_pos * pages
     count = sel.shape[1]
@@ -187,18 +235,6 @@
         w = jnp.exp(scores[i] - peak)
         total = total + w
         wbuf[i * rows : (i + 1) * rows, :] = w.astype(BF)
-    land_w = jnp.exp(land - peak)
-    recent_w = jnp.exp(recent - peak)
-    row_sum = jnp.sum(total + land_w, axis=1, keepdims=True) + jnp.sum(
-        recent_w, axis=1, keepdims=True
-    )
-    acc_out[...] = diagonal(
-        nn(land_w.astype(BF), sum_ref[...]) + nn(recent_w.astype(BF), rv_ref[...]), heads, gqa
-    )
-    at_lane = iota((rows, LANES), 0) == iota((rows, LANES), 1)
-    stat_out[0:1, :] = jnp.sum(jnp.where(at_lane, peak, 0.0), axis=0, keepdims=True)
-    stat_out[1:2, :] = jnp.sum(jnp.where(at_lane, row_sum, 0.0), axis=0, keepdims=True)
-    stat_out[2:8, :] = jnp.zeros((6, LANES), F32)
 
     owners = own_ref[...]
     before = nn(
@@ -213,6 +249,8 @@
         page = (iota((1, LANES), 1) + c * LANES).astype(F32)
         slots.append(jnp.where(owners[c : c + 1, :] == 1, ones + pages // 2, page - ones))
     slot = jnp.concatenate(slots, axis=1).astype(jnp.int32)
+    slot = slot - (1 - core) * (pages // 2)
+    slot = jnp.where(slot < 0, slot + pages, slot)
     onehot[...] = ones_where(iota((pages, pages), 0) == slot)
     moved = nt(wbuf[...], onehot[...]).astype(BF)
     for c in range(chunks):
@@ -220,59 +258,10 @@
             grouped[c * rows : (c + 1) * rows, i * LANES : (i + 1) * LANES] = moved[
                 i * rows : (i + 1) * rows, c * LANES : (c + 1) * LANES
             ]
-    span = LANES * PAGE
     col = iota((1, span), 1)
     perm[...] = ones_where(iota((span, span), 0) == col % PAGE * LANES + col // PAGE)
-    w_out[...] = nn(grouped[...], perm[...]).astype(BF)
-
-
-def merge_kernel(
-    heads,
-    seq_count,
-    w_ref,
-    acc_ref,
-    stat_ref,
-    pool_ref,
-    out_ref,
-    values,
-    theirs,
-    back_out,
-    back_in,
-    message,
-    gathered,
-    v_sem,
-    pair_send,
-    pair_recv,
-    send_sem,
-    recv_sem,
-):
-    seq_pos = lax.axis_index("seq")
-    core = lax.axis_index("pool")
-    rows = acc_ref.shape[0]
-    gqa = rows // heads
-    width = heads * HD
-    span = LANES * PAGE
-    parts = pool_ref.shape[0] // span
-    partner = {"pool": 1 - core}
-
-    loads = []
-    for g in range(parts):
-        load = pltpu.make_async_copy(
-            pool_ref.at[pl.ds(g * span, span), :], values.at[pl.ds(g * span, span), :], v_sem.at[g]
-        )
-        load.start()
-        loads.append(load)
-
-    barrier = pltpu.get_barrier_semaphore()
-    pl.semaphore_signal(barrier, inc=1, device_id=partner, device_id_type=MESH)
-    for k in range(1, seq_count):
-        pl.semaphore_signal(
-            barrier,
-            inc=1,
-            device_id={"seq": lax.rem(seq_pos + k, seq_count)},
-            device_id_type=MESH,
-        )
-    pl.semaphore_wait(barrier, seq_count)
+    half = parts * rows
+    outgoing[...] = nn(grouped[0:half, :], perm[...]).astype(BF)
 
     def pair_copy(src, dst, n):
         return pltpu.make_async_remote_copy(
@@ -284,19 +273,32 @@
             device_id_type=MESH,
         )
 
-    half = parts * rows
-    swap = pair_copy(w_ref.at[pl.ds(pl.multiple_of((1 - core) * half, 32), half), :], theirs, 0)
+    pl.semaphore_wait(barrier, seq_count)
+    swap = pair_copy(outgoing, theirs, 0)
     swap.start()
+    own_w = nn(grouped[half : 2 * half, :], perm[...]).astype(BF)
+
+    land_w = jnp.exp(land - peak)
+    recent_w = jnp.exp(recent - peak)
+    row_sum = jnp.sum(total + land_w, axis=1, keepdims=True) + jnp.sum(
+        recent_w, axis=1, keepdims=True
+    )
+    at_lane = iota((rows, LANES), 0) == iota((rows, LANES), 1)
+    message[rows : rows + 1, :] = jnp.sum(jnp.where(at_lane, peak, 0.0), axis=0, keepdims=True)
+    message[rows + 1 : rows + 2, :] = jnp.sum(
+        jnp.where(at_lane, row_sum, 0.0), axis=0, keepdims=True
+    )
+    message[rows + 2 : rows + 8, :] = jnp.zeros((6, LANES), F32)
+    sum_load.wait()
+    mine = nn(land_w.astype(BF), summary[...]) + nn(recent_w.astype(BF), rv_ref[...])
 
     def weighted(weights, columns, g):
         return nn(weights, values[g * span : (g + 1) * span, columns])
 
-    mine = jnp.zeros((rows, width), F32)
     my_cols = pl.ds(pl.multiple_of(core * width, width), width)
     for g in range(parts):
         loads[g].wait()
-        w = w_ref[pl.ds(pl.multiple_of(core * half + g * rows, 32), rows), :]
-        mine = mine + weighted(w, my_cols, g)
+        mine = mine + weighted(own_w[g * rows : (g + 1) * rows, :], my_cols, g)
     swap.wait()
     other = jnp.zeros((rows, width), F32)
     other_cols = pl.ds(pl.multiple_of((1 - core) * width, width), width)
@@ -305,8 +307,7 @@
     back_out[...] = diagonal(other, heads, gqa)
     back = pair_copy(back_out, back_in, 1)
     back.start()
-    part = acc_ref[...] + diagonal(mine, heads, gqa)
-    message[rows : rows + 8, :] = stat_ref[...]
+    part = diagonal(mine, heads, gqa)
     back.wait()
     message[0:rows, :] = part + back_in[...]
 
@@ -331,7 +332,6 @@
         peaks.append(gathered[k, rows : rows + 1, :])
         sums.append(gathered[k, rows + 1 : rows + 2, :])
     joint = functools.reduce(jnp.maximum, peaks)
-    at_lane = iota((rows, LANES), 0) == iota((rows, LANES), 1)
 
     def column(row):
         return jnp.sum(jnp.where(at_lane, row, 0.0), axis=1, keepdims=True)
@@ -343,7 +343,8 @@
         weight_sum = weight_sum + sums[k] * factor
         body = message[0:rows, :] if k == 0 else gathered[k - 1, 0:rows, :]
         mixed = mixed + body * column(factor)
-    out_ref[...] = (mixed / column(weight_sum)).astype(BF)
+    result = mixed / column(weight_sum)
+    out_ref[...] = jnp.concatenate([result[r : r + 1, :] for r in range(rows)], axis=1).astype(BF)
 
 
 def local(
@@ -366,18 +367,19 @@
     pages = tokens // PAGE
     chunks = pages // LANES
     span = LANES * PAGE
+    parts = value_pool.shape[1] // span
     tables = [jnp.asarray(t) for t in angle_tables(tokens * seq_count, HD)]
     vmem = pl.BlockSpec(memory_space=pltpu.VMEM)
-    weights, acc, stats = pl.pallas_call(
-        functools.partial(local_kernel, heads),
-        out_shape=(
-            jax.ShapeDtypeStruct((chunks * rows, span), BF),
-            jax.ShapeDtypeStruct((rows, LANES), F32),
-            jax.ShapeDtypeStruct((8, LANES), F32),
-        ),
-        in_specs=[pl.BlockSpec(memory_space=pltpu.SMEM)] + [vmem] * 12,
-        out_specs=(vmem, vmem, vmem),
+    hbm = pl.BlockSpec(memory_space=pl.ANY)
+    return pl.pallas_call(
+        functools.partial(attention_kernel, heads, seq_count),
+        out_shape=jax.ShapeDtypeStruct((1, rows * HD), BF),
+        in_specs=[pl.BlockSpec(memory_space=pltpu.SMEM)] + [vmem] * 10 + [hbm] * 3,
+        out_specs=vmem,
         scratch_shapes=[
+            pltpu.VMEM((rank_dim, tokens), BF),
+            pltpu.VMEM((pages, width), BF),
+            pltpu.VMEM(value_pool.shape[1:], BF),
             pltpu.VMEM((PAGE, pages, width), BF),
             pltpu.VMEM((pages, width), BF),
             pltpu.VMEM((PAGE, rows, pages), F32),
@@ -385,33 +387,14 @@
             pltpu.VMEM((pages, pages), BF),
             pltpu.VMEM((chunks * rows, span), BF),
             pltpu.VMEM((span, span), BF),
-        ],
-        compiler_params=pltpu.CompilerParams(vmem_limit_bytes=60 * 1024 * 1024),
-    )(
-        lengths,
-        factors[0],
-        basis[0],
-        page_summary[0],
-        recent_keys[0],
-        recent_values[0],
-        query.reshape(rows, HD),
-        selected[0],
-        owner_map.reshape(chunks, LANES),
-        *tables,
-    )
-    parts = value_pool.shape[1] // span
-    out = pl.pallas_call(
-        functools.partial(merge_kernel, heads, seq_count),
-        out_shape=jax.ShapeDtypeStruct((rows, HD), BF),
-        in_specs=[vmem, vmem, vmem, pl.BlockSpec(memory_space=pl.ANY)],
-        out_specs=vmem,
-        scratch_shapes=[
-            pltpu.VMEM(value_pool.shape[1:], BF),
+            pltpu.VMEM((parts * rows, span), BF),
             pltpu.VMEM((parts * rows, span), BF),
             pltpu.VMEM((rows, LANES), F32),
             pltpu.VMEM((rows, LANES), F32),
             pltpu.VMEM((rows + 8, LANES), F32),
             pltpu.VMEM((seq_count - 1, rows + 8, LANES), F32),
+            pltpu.SemaphoreType.DMA((chunks,)),
+            pltpu.SemaphoreType.DMA,
             pltpu.SemaphoreType.DMA((parts,)),
             pltpu.SemaphoreType.DMA((2,)),
             pltpu.SemaphoreType.DMA((2,)),
@@ -419,10 +402,21 @@
             pltpu.SemaphoreType.DMA((seq_count - 1,)),
         ],
         compiler_params=pltpu.CompilerParams(
-            collective_id=0, has_side_effects=True, vmem_limit_bytes=40 * 1024 * 1024
+            collective_id=0, has_side_effects=True, vmem_limit_bytes=60 * 1024 * 1024
         ),
-    )(weights, acc, stats, value_pool[0])
-    return out.reshape(1, rows * HD)
+    )(
+        lengths,
+        basis[0],
+        recent_keys[0],
+        recent_values[0],
+        query,
+        selected[0],
+        owner_map.reshape(chunks, LANES),
+        *tables,
+        jnp.swapaxes(factors[0], 0, 1),
+        page_summary[0],
+        value_pool[0],
+    )
 
 
 def solution(mesh):

time: 47.3 us -> 31.5 us (0.67)
  local copies, waits for them, and re-layouts: 12.1 us -> 1.34 us
  Pallas kernels: 32.7 us -> 29.2 us
  other arithmetic: 1.36 us -> 0 us
    unnamed x10 -> x1, local copies, waits for them, and re-layouts: 12.1 us -> 1.34 us
    pallas_call x2 -> x1, Pallas kernels: 32.7 us -> 29.2 us  [local(): pl.pallas_call(functools.partial(attention_kernel, heads, seq_count), out...]
    unnamed x1 -> x0, other arithmetic: 1.36 us -> none
where the time goes in v2:
time: 31.5 us; the launch traced here: 31.2 us
  Pallas kernels  29.2 us (93%)
  local copies, waits for them, and re-layouts  1.34 us (4%)
  between operations  0.66 us (2%)
    pallas_call x1, Pallas kernels, local(): pl.pallas_call(functools.partial(attention_kernel, heads, seq_count), out...  29.2 us
    unnamed x1, local copies, waits for them, and re-layouts  1.34 us

profile of v2, /device:TPU:0, one launch (start us, length us, event | category | flops | bytes accessed | tf_op | source)
XLA Modules:
  0.0 31.2 jit_solution(4210283623645779066)
XLA Ops:
  0.7 29.2 %shard_map.136 = bf16[1,4096]{1,0:T(2,128)(2,1)} custom-call(s32[1]{0:T(128)S(6)} %copy.16.len_ref, bf16[160,512]{1,0:T(8,128)(2,1)} %bitcast.13, bf16[64,512]{1,0:T(8,128)(2,1)} %bitcast.14, bf16[64,512]{1,0:T(8,128)(2,1)} %bitcast.15, bf16[1,4096]{1,0:T(2,128)(2,1)} %q_ref.1, s32[8,1024]{1,0:T(8,128)} %bitcast.16, s32[8,128]{1,0:T(8,128)} %bitcast.17, ...), custom_call_target="tpu_custom_call" | custom-call | tf_op jit(solution)/shard_map/pallas_call | solution.py:374
  29.9 1.3 %copy.17 = bf16[1,4096]{1,0:T(2,128)(2,1)} copy(bf16[1,4096]{1,0:T(2,128)(2,1)} %shard_map.136) | data formatting | bytes 16384

commit v3 on v2

--- a/solution.py
+++ b/solution.py
@@ -95,8 +95,8 @@
     theirs,
     back_out,
     back_in,
-    message,
-    gathered,
+    bodies,
+    stats,
     f_sem,
     s_sem,
     v_sem,
@@ -193,16 +193,6 @@
             mid = (low[n].astype(BF).astype(F32) + high[n].astype(BF).astype(F32)) * 0.5
             centers[at, n * LANES : (n + 1) * LANES] = jnp.where(any_live, mid, 0.0).astype(BF)
 
-    per_chunk = span // FINE
-
-    def step(t, carry):
-        fac_load(t).wait()
-        for k in range(per_chunk):
-            block(t * per_chunk + k)
-        return carry
-
-    lax.fori_loop(0, chunks, step, 0)
-
     sel = jnp.where(core == 0, sel_ref[:heads, :], sel_ref[heads:, :]) - seq_pos * pages
     count = sel.shape[1]
     masks = []
@@ -216,26 +206,6 @@
         row = jnp.concatenate([hit[c : c + 1, :] for c in range(chunks)], axis=1)
         masks.append(jnp.broadcast_to(row, (gqa, pages)))
     chosen = jnp.concatenate(masks, axis=0) > 0.5
-    page_tok = iota((rows, pages), 1) * PAGE
-    land = nt(q_perm, centers[...]) * scale
-    land = jnp.where((page_tok < limit) & jnp.logical_not(chosen), land, -jnp.inf)
-    recent = nt(q_plain, rk_ref[...]) * scale
-    first = jnp.zeros(recent.shape, jnp.int32) + seq_pos
-    recent = jnp.where(first == 0, recent, -jnp.inf)
-    peak = jnp.maximum(jnp.max(land, axis=1, keepdims=True), jnp.max(recent, axis=1, keepdims=True))
-    top = jnp.full((rows, pages), -1e30, F32)
-    for i in range(PAGE):
-        s = nt(q_perm, keys[i]) * scale
-        s = jnp.where((page_tok + i < limit) & chosen, s, -jnp.inf)
-        scores[i] = s
-        top = jnp.maximum(top, s)
-    peak = jnp.maximum(peak, jnp.max(top, axis=1, keepdims=True))
-    total = jnp.zeros((rows, pages), F32)
-    for i in range(PAGE):
-        w = jnp.exp(scores[i] - peak)
-        total = total + w
-        wbuf[i * rows : (i + 1) * rows, :] = w.astype(BF)
-
     owners = own_ref[...]
     before = nn(
         ones_where(owners == 1), ones_where(iota((LANES, LANES), 0) < iota((LANES, LANES), 1))
@@ -251,15 +221,47 @@
     slot = jnp.concatenate(slots, axis=1).astype(jnp.int32)
     slot = slot - (1 - core) * (pages // 2)
     slot = jnp.where(slot < 0, slot + pages, slot)
-    onehot[...] = ones_where(iota((pages, pages), 0) == slot)
+    per_chunk = span // FINE
+
+    def step(t, carry):
+        fac_load(t).wait()
+        for k in range(per_chunk):
+            block(t * per_chunk + k)
+        return carry
+
+    lax.fori_loop(0, chunks, step, 0)
+
+    page_tok = iota((rows, pages), 1) * PAGE
+    land = nt(q_perm, centers[...]) * scale
+    land = jnp.where((page_tok < limit) & jnp.logical_not(chosen), land, -jnp.inf)
+    recent = nt(q_plain, rk_ref[...]) * scale
+    first = jnp.zeros(recent.shape, jnp.int32) + seq_pos
+    recent = jnp.where(first == 0, recent, -jnp.inf)
+    peak = jnp.maximum(jnp.max(land, axis=1, keepdims=True), jnp.max(recent, axis=1, keepdims=True))
+    top = jnp.full((rows, pages), -1e30, F32)
+    col = iota((1, span), 1)
+    target = col % PAGE * LANES + col // PAGE
+    for i in range(PAGE):
+        s = nt(q_perm, keys[i]) * scale
+        for full, ref, goal in ((pages, onehot, slot), (span, perm, target)):
+            n = full // PAGE
+            ref[i * n : (i + 1) * n, :] = ones_where(iota((n, full), 0) == goal - i * n)
+        s = jnp.where((page_tok + i < limit) & chosen, s, -jnp.inf)
+        scores[i] = s
+        top = jnp.maximum(top, s)
+    peak = jnp.maximum(peak, jnp.max(top, axis=1, keepdims=True))
+    total = jnp.zeros((rows, pages), F32)
+    for i in range(PAGE):
+        w = jnp.exp(scores[i] - peak)
+        total = total + w
+        wbuf[i * rows : (i + 1) * rows, :] = w.astype(BF)
+
     moved = nt(wbuf[...], onehot[...]).astype(BF)
     for c in range(chunks):
         for i in range(PAGE):
             grouped[c * rows : (c + 1) * rows, i * LANES : (i + 1) * LANES] = moved[
                 i * rows : (i + 1) * rows, c * LANES : (c + 1) * LANES
             ]
-    col = iota((1, span), 1)
-    perm[...] = ones_where(iota((span, span), 0) == col % PAGE * LANES + col // PAGE)
     half = parts * rows
     outgoing[...] = nn(grouped[0:half, :], perm[...]).astype(BF)
 
@@ -273,6 +275,21 @@
             device_id_type=MESH,
         )
 
+    def spread(ref, n):
+        started = []
+        for k in range(1, seq_count):
+            send = pltpu.make_async_remote_copy(
+                src_ref=ref.at[seq_pos],
+                dst_ref=ref.at[seq_pos],
+                send_sem=send_sem.at[n, k - 1],
+                recv_sem=recv_sem.at[n, k - 1],
+                device_id={"seq": lax.rem(seq_pos + k, seq_count)},
+                device_id_type=MESH,
+            )
+            send.start()
+            started.append(send)
+        return started
+
     pl.semaphore_wait(barrier, seq_count)
     swap = pair_copy(outgoing, theirs, 0)
     swap.start()
@@ -284,11 +301,11 @@
         recent_w, axis=1, keepdims=True
     )
     at_lane = iota((rows, LANES), 0) == iota((rows, LANES), 1)
-    message[rows : rows + 1, :] = jnp.sum(jnp.where(at_lane, peak, 0.0), axis=0, keepdims=True)
-    message[rows + 1 : rows + 2, :] = jnp.sum(
-        jnp.where(at_lane, row_sum, 0.0), axis=0, keepdims=True
-    )
-    message[rows + 2 : rows + 8, :] = jnp.zeros((6, LANES), F32)
+    as_rows = [
+        jnp.sum(jnp.where(at_lane, col_of, 0.0), axis=0, keepdims=True) for col_of in (peak, row_sum)
+    ]
+    stats[seq_pos] = jnp.concatenate(as_rows + [jnp.zeros((6, LANES), F32)], axis=0)
+    sends = spread(stats, 0)
     sum_load.wait()
     mine = nn(land_w.astype(BF), summary[...]) + nn(recent_w.astype(BF), rv_ref[...])
 
@@ -309,28 +326,13 @@
     back.start()
     part = diagonal(mine, heads, gqa)
     back.wait()
-    message[0:rows, :] = part + back_in[...]
-
-    sends = []
-    for k in range(1, seq_count):
-        send = pltpu.make_async_remote_copy(
-            src_ref=message,
-            dst_ref=gathered.at[k - 1],
-            send_sem=send_sem.at[k - 1],
-            recv_sem=recv_sem.at[k - 1],
-            device_id={"seq": lax.rem(seq_pos + k, seq_count)},
-            device_id_type=MESH,
-        )
-        send.start()
-        sends.append(send)
+    bodies[seq_pos] = (part + back_in[...]).astype(BF)
+    sends = sends + spread(bodies, 1)
     for send in sends:
         send.wait()
 
-    peaks = [message[rows : rows + 1, :]]
-    sums = [message[rows + 1 : rows + 2, :]]
-    for k in range(seq_count - 1):
-        peaks.append(gathered[k, rows : rows + 1, :])
-        sums.append(gathered[k, rows + 1 : rows + 2, :])
+    peaks = [stats[k, 0:1, :] for k in range(seq_count)]
+    sums = [stats[k, 1:2, :] for k in range(seq_count)]
     joint = functools.reduce(jnp.maximum, peaks)
 
     def column(row):
@@ -341,8 +343,7 @@
     for k in range(seq_count):
         factor = jnp.exp(peaks[k] - joint)
         weight_sum = weight_sum + sums[k] * factor
-        body = message[0:rows, :] if k == 0 else gathered[k - 1, 0:rows, :]
-        mixed = mixed + body * column(factor)
+        mixed = mixed + bodies[k].astype(F32) * column(factor)
     result = mixed / column(weight_sum)
     out_ref[...] = jnp.concatenate([result[r : r + 1, :] for r in range(rows)], axis=1).astype(BF)
 
@@ -391,15 +392,15 @@
             pltpu.VMEM((parts * rows, span), BF),
             pltpu.VMEM((rows, LANES), F32),
             pltpu.VMEM((rows, LANES), F32),
-            pltpu.VMEM((rows + 8, LANES), F32),
-            pltpu.VMEM((seq_count - 1, rows + 8, LANES), F32),
+            pltpu.VMEM((seq_count, rows, LANES), BF),
+            pltpu.VMEM((seq_count, 8, LANES), F32),
             pltpu.SemaphoreType.DMA((chunks,)),
             pltpu.SemaphoreType.DMA,
             pltpu.SemaphoreType.DMA((parts,)),
             pltpu.SemaphoreType.DMA((2,)),
             pltpu.SemaphoreType.DMA((2,)),
-            pltpu.SemaphoreType.DMA((seq_count - 1,)),
-            pltpu.SemaphoreType.DMA((seq_count - 1,)),
+            pltpu.SemaphoreType.DMA((2, seq_count - 1)),
+            pltpu.SemaphoreType.DMA((2, seq_count - 1)),
         ],
         compiler_params=pltpu.CompilerParams(
             collective_id=0, has_side_effects=True, vmem_limit_bytes=60 * 1024 * 1024

time: 31.5 us -> 30.9 us (0.981)
  Pallas kernels: 29.2 us -> 28.7 us
    pallas_call x1, Pallas kernels: 29.2 us -> 28.7 us  [local(): pl.pallas_call(functools.partial(attention_kernel, heads, seq_count), out...]
where the time goes in v3:
time: 30.9 us; the launch traced here: 30.7 us
  Pallas kernels  28.7 us (93%)
  local copies, waits for them, and re-layouts  1.34 us (4%)
  between operations  0.66 us (2%)
    pallas_call x1, Pallas kernels, local(): pl.pallas_call(functools.partial(attention_kernel, heads, seq_count), out...  28.7 us
    unnamed x1, local copies, waits for them, and re-layouts  1.34 us

profile of v3, /device:TPU:0, one launch (start us, length us, event | category | flops | bytes accessed | tf_op | source)
XLA Modules:
  0.0 30.7 jit_solution(7395999219452300782)
XLA Ops:
  0.7 28.7 %shard_map.136 = bf16[1,4096]{1,0:T(2,128)(2,1)} custom-call(s32[1]{0:T(128)S(6)} %copy.16.len_ref, bf16[160,512]{1,0:T(8,128)(2,1)} %bitcast.13, bf16[64,512]{1,0:T(8,128)(2,1)} %bitcast.14, bf16[64,512]{1,0:T(8,128)(2,1)} %bitcast.15, bf16[1,4096]{1,0:T(2,128)(2,1)} %q_ref.1, s32[8,1024]{1,0:T(8,128)} %bitcast.16, s32[8,128]{1,0:T(8,128)} %bitcast.17, ...), custom_call_target="tpu_custom_call" | custom-call | tf_op jit(solution)/shard_map/pallas_call | solution.py:375
  29.3 1.3 %copy.17 = bf16[1,4096]{1,0:T(2,128)(2,1)} copy(bf16[1,4096]{1,0:T(2,128)(2,1)} %shard_map.136) | data formatting | bytes 16384
